TPU v7x, 32 devices: a whole 2x2x4 slice. The times are simulated.
32 devices in a mesh: row: 4 (over x, core), col: 2 (over y), fiber: 4 (over z).
Axes of the slice: x: 2, y: 2, z: 4, core: 2. Of those that a mesh axis runs over, the one named last changes fastest.
Arguments:
- values: float32 [3072, 3072], P('row', ('col', 'fiber')), may hold values from -6 to 6
- tile_mask: int32 [24, 24], P('row', ('col', 'fiber')), may hold values from 0 to 1, as said below
- keep_mask: int32 [24, 24], P('row', ('col', 'fiber')), may hold values 0 or 1
Outputs:
- flows: float32 [3072, 3072], P('row', ('col', 'fiber'))
Inputs may be any that keep to these rules, and one draw needn't show every extreme that they name: `tile_mask`: 1 marks a tile that holds entries; every diagonal tile is 1, and tiles with low indices are denser.
All inputs are finite; a program needn't handle non-finite values. No bound on the sum of `keep_mask` on one device may be relied on, other than what follows from the above.
Results may differ from a plain program's by a relative error of at most 0.017.
Values may be sent and summed in bfloat16 or wider, within the bound.
A program may use at most 64 MiB of HBM per device.

v0:
```python
import jax
import jax.numpy as jnp
from jax import lax
from jax.sharding import PartitionSpec as P


def spread_tiles(mask, tile_size):
    count_rows, count_cols = mask.shape
    wide = jnp.broadcast_to(
        mask.astype(jnp.float32)[:, None, :, None], (count_rows, tile_size, count_cols, tile_size)
    )
    return wide.reshape(count_rows * tile_size, count_cols * tile_size)


def local(values, tile_mask, keep_mask):
    n_row = lax.axis_size("row")
    n_fib = lax.axis_size("fiber")
    tile_size = values.shape[1] // tile_mask.shape[1]
    weighted = (values * spread_tiles(tile_mask, tile_size)).astype(jnp.bfloat16)
    rows_dev, unit_width = weighted.shape
    sub_width = unit_width // n_fib
    unit_count = rows_dev // unit_width
    left_stack = weighted.reshape(rows_dev, n_fib, sub_width)
    right_stack = weighted.reshape(unit_count, n_fib, sub_width, unit_width)
    left_recv, right_recv = (
        lax.all_to_all(left_stack, "fiber", split_axis=1, concat_axis=1, tiled=True),
        lax.all_to_all(right_stack, "fiber", split_axis=1, concat_axis=1, tiled=True),
    )
    left_local = left_recv.reshape(rows_dev, unit_width)
    right_local = jnp.transpose(right_recv, (0, 2, 1, 3)).reshape(
        unit_count * sub_width, n_fib * unit_width
    )
    left_all = lax.all_gather(left_local, "col", axis=1, tiled=True)
    partial_product = jnp.dot(
        left_all,
        lax.all_gather(right_local, "row", axis=0, tiled=True),
        preferred_element_type=jnp.float32,
    )
    expanded = lax.psum_scatter(
        partial_product.astype(jnp.bfloat16), "fiber", scatter_dimension=1, tiled=True
    ).astype(jnp.float32)
    squared = expanded * expanded
    col_total = lax.psum(jnp.sum(squared, axis=0), "row")
    col_scale = col_total / (rows_dev * n_row) + 1e-06
    return spread_tiles(keep_mask, tile_size) * squared / col_scale[None, :]


def solution(mesh):
    return jax.shard_map(
        local,
        mesh=mesh,
        in_specs=(
            P("row", ("col", "fiber")),
            P("row", ("col", "fiber")),
            P("row", ("col", "fiber")),
        ),
        out_specs=P("row", ("col", "fiber")),
        check_vma=False,
    )
```

profile of v0, /device:TPU:0, one launch (start us, length us, event | category | flops | bytes accessed | tf_op | source)
XLA Modules:
  0.0 149.5 jit_solution(16989294476739520864)
XLA Ops:
  6.5 0.0 all-gather.3.cloned.1.call-start
  6.5 0.7 convert_element_type.16
  7.2 1.6 %copy.13 = f32[768,384]{0,1:T(8,128)S(1)} copy(f32[768,384]{1,0:T(8,128)} %param.3) | data formatting | bytes 2359296 | tf_op args[0]
  8.9 0.2 broadcast_in_dim.5
  9.0 0.4 fusion
  9.4 22.1 %all_to_all.10 = bf16[768,4,96]{0,2,1:T(8,128)(2,1)} all-to-all(bf16[768,4,96]{0,2,1:T(8,128)(2,1)S(1)} %bitcast.32), channel_id=1, replica_groups=mesh['row'=4,'col'=2,'fiber'=4] {'fiber'}, dimensions={1} | all-to-all | bytes 1179648 | tf_op jit(solution)/shard_map/all_to_all | solution.py:26
  31.6 0.0 all-gather.3.cloned.1.call-update
  31.6 0.0 all-gather.5.cloned.1.call-start
  31.6 0.3 copy.14
  31.9 0.1 copy.15
  32.0 17.8 %all_to_all.11 = bf16[2,4,96,384]{3,2,0,1:T(8,128)(2,1)S(1)} all-to-all(bf16[2,4,96,384]{3,2,0,1:T(8,128)(2,1)S(1)} %copy.15), channel_id=1, replica_groups=mesh['row'=4,'col'=2,'fiber'=4] {'fiber'}, dimensions={1} | all-to-all | bytes 1179648 | tf_op jit(solution)/shard_map/all_to_all | solution.py:27
  49.8 0.5 copy.16
  50.2 0.9 copy.23
  51.1 0.0 all-gather.5.cloned.1.call-update
  51.2 0.0 reduce-scatter.4.cloned.1.call-start
  51.2 2.4 %all-gather.3.cloned.1.call-done = bf16[768,768]{0,1:T(8,128)(2,1)} async-done(((bf16[768,384]{0,1:T(8,128)(2,1)}), bf16[768,768]{0,1:T(8,128)(2,1)}) %all-gather.3.cloned.1.call-update) | async-done | bytes 1179664 | tf_op jit(solution)/shard_map/all_gather | solution.py:33
  53.6 25.6 %all-gather.5.cloned.1.call-done = bf16[768,1536]{1,0:T(8,128)(2,1)} async-done(((bf16[192,1536]{1,0:T(8,128)(2,1)}), bf16[768,1536]{1,0:T(8,128)(2,1)}) %all-gather.5.cloned.1.call-update) | async-done | bytes 2359312 | tf_op jit(solution)/shard_map/all_gather | solution.py:36
  79.2 4.1 %convolution_convert_fusion = bf16[768,1536]{1,0:T(8,128)(2,1)S(1)} fusion(bf16[768,768]{0,1:T(8,128)(2,1)} %all-gather.3.cloned.1.call-done, bf16[768,1536]{1,0:T(8,128)(2,1)} %all-gather.5.cloned.1.call-done), kind=kOutput, calls=%fused_computation | convolution fusion | flops 1813118976 | bytes 5898240 | tf_op jit(solution)/shard_map/dot_general | solution.py:34
  83.3 2.5 %copy.19 = bf16[768,1536]{0,1:T(8,128)(2,1)} copy(bf16[768,1536]{1,0:T(8,128)(2,1)S(1)} %convolution_convert_fusion) | data formatting | bytes 4718592
  85.8 0.0 copy-start.1
  85.8 0.0 reduce-scatter.4.cloned.1.call-update
  85.8 0.7 copy-done.1
  86.4 47.2 %reduce-scatter.4.cloned.1.call-done = bf16[384,768]{1,0:T(8,128)(2,1)} async-done(((bf16[1536,768]{1,0:T(8,128)(2,1)}), bf16[384,768]{1,0:T(8,128)(2,1)}) %reduce-scatter.4.cloned.1.call-update) | async-done | bytes 589840
  133.6 0.0 copy-start
  133.6 1.3 fusion.2
  135.0 6.2 %psum.7 = f32[384]{0:T(512)S(1)} all-reduce(f32[384]{0:T(512)S(1)} %fusion.2), channel_id=1, replica_groups=mesh['row'=4,'col'=2,'fiber'=4] {'row'}, use_global_device_ids=true, to_apply=%region_2.0 | all-reduce | flops 384 | bytes 3072 | tf_op jit(solution)/shard_map/psum | solution.py:43
  141.1 0.2 broadcast_in_dim.4
  141.3 0.0 copy-done
  141.3 0.2 fusion.1
  141.6 1.4 copy.18
  (2 shorter events, 0.0 us)
Async XLA Ops:
  6.5 47.1 %all-gather.3.cloned.1.call-start = ((), (), s32[]{:S(2)}) async-start(), calls=%async_computation.3 | async-start | bytes 1769472 | tf_op jit(solution)/shard_map/all_gather | solution.py:33
  31.6 47.7 %all-gather.5.cloned.1.call-start = ((), (), s32[]{:S(2)}) async-start(), calls=%async_computation.4 | async-start | bytes 2949120 | tf_op jit(solution)/shard_map/all_gather | solution.py:36
  51.2 82.5 %reduce-scatter.4.cloned.1.call-start = ((), (), s32[]{:S(2)}) async-start(), calls=%async_computation.5 | async-start | bytes 2949120
  85.8 0.7 copy-start.1
  133.6 7.7 %copy-start = (bf16[384,768]{1,0:T(8,128)(2,1)S(1)}, bf16[384,768]{1,0:T(8,128)(2,1)}, u32[]{:S(2)}) copy-start(bf16[384,768]{1,0:T(8,128)(2,1)} %reduce-scatter.4.cloned.1.call-done) | copy-start | bytes 1769476
Sparse Core Ops, SparseCore 0:
  31.7 21.8 all-gather.2
  55.2 24.0 all-gather.4
  85.9 47.6 reduce-scatter.3
where the time goes:
time: 150 us; the launch traced here: 149 us
  waiting for transfers between devices  75.3 us (50%)
  blocking collectives  46.1 us (31%)
  between operations  13.2 us (9%)
  local copies, waits for them, and re-layouts  8.19 us (5%)
  matrix products  4.05 us (3%)
  other arithmetic  2.63 us (2%)
    unnamed x4, waiting for transfers between devices  47.2 us
    all_gather x1, waiting for transfers between devices, local(): lax.all_gather(right_local, 'row', axis=0, tiled=True)  25.6 us
    all_to_all x1, blocking collectives, local(): lax.all_to_all(left_stack, 'fiber', split_axis=1, concat_axis=1, tiled=True)  22.1 us
    all_to_all x1, blocking collectives, local(): lax.all_to_all(right_stack, 'fiber', split_axis=1, concat_axis=1, tiled=T...  17.8 us
    psum x1, blocking collectives, local(): col_total = lax.psum(jnp.sum(squared, axis=0), 'row')  6.17 us
    unnamed x7, local copies, waits for them, and re-layouts  5.65 us
    dot_general x1, matrix products, local(): jnp.dot(left_all, lax.all_gather(right_local, 'row', axis=0, tiled=True),...  4.05 us
  transfers between devices with their start and end apart: 3, of which 3 were waited for; matrix products, arithmetic and copies ran while one was open for 1% of the time, Pallas kernels for 0%

commit v1 on v0

v1 whole, which is shorter than its diff:
```python
import functools

import jax
import jax.numpy as jnp
from jax import lax
from jax.experimental import pallas as pl
from jax.experimental.pallas import tpu as pltpu
from jax.sharding import PartitionSpec as P

MESH = pl.DeviceIdType.MESH
CHUNKS = 4


def kernel(
    n_row, n_col, n_fib, tile_ref, keep_ref, values_ref, out_ref,
    left, right, own, part_out, part_in, sums,
    send_up, send_down, recv_left, send_right, recv_right, send_pair, recv_pair,
    send_part, recv_part, send_sum, recv_sum,
):
    r, c, f = lax.axis_index("row"), lax.axis_index("col"), lax.axis_index("fiber")
    rows, unit = values_ref.shape
    tile = unit // tile_ref.shape[1]
    step = rows // CHUNKS
    group = n_row // n_col
    owner, seat = r // group, lax.rem(r, group)

    barrier = pltpu.get_barrier_semaphore()
    for dr in range(n_row):
        for dc in range(n_col):
            if dr or dc:
                pl.semaphore_signal(
                    barrier, inc=1, device_id_type=MESH,
                    device_id=(lax.rem(r + dr, n_row), lax.rem(c + dc, n_col), f),
                )

    has_down, has_up = f > 0, f < n_fib - 1

    @pl.when(has_down)
    def _():
        pl.semaphore_signal(barrier, inc=1, device_id=(r, c, f - 1), device_id_type=MESH)

    @pl.when(has_up)
    def _():
        pl.semaphore_signal(barrier, inc=1, device_id=(r, c, f + 1), device_id_type=MESH)

    for i in range(rows // tile):
        for j in range(unit // tile):
            at = (pl.ds(i * tile, tile), pl.ds(j * tile, tile))
            masked = values_ref[at] * tile_ref[i, j].astype(jnp.float32)
            left[f, i * tile:(i + 1) * tile, j * tile:(j + 1) * tile] = masked.astype(jnp.bfloat16)

    neighbours = has_down.astype(jnp.int32) + has_up.astype(jnp.int32)
    pl.semaphore_wait(barrier, n_row * n_col - 1 + neighbours)

    def along(source, i, up):
        part = left.at[source, pl.ds(pl.multiple_of(i * step, step), step)]
        return pltpu.make_async_remote_copy(
            src_ref=part, dst_ref=part,
            send_sem=(send_up if up else send_down).at[source, i],
            recv_sem=recv_left.at[source, i],
            device_id=(r, c, f + 1 if up else f - 1), device_id_type=MESH,
        )

    def right_at(col, place):
        return right.at[
            pl.ds(pl.multiple_of(place * rows, rows), rows),
            pl.ds(pl.multiple_of(col * unit, unit), unit),
        ]

    def to_right(t):
        return pltpu.make_async_remote_copy(
            src_ref=left.at[f], dst_ref=right_at(c, seat),
            send_sem=send_right.at[t], recv_sem=recv_right.at[c],
            device_id=(t * group + seat, owner, f), device_id_type=MESH,
        )

    def came_right(col):
        return pltpu.make_async_remote_copy(
            src_ref=left.at[f], dst_ref=right_at(col, seat),
            send_sem=send_right.at[0], recv_sem=recv_right.at[col],
            device_id=(r, c, f), device_id_type=MESH,
        )

    def to_pair(col, other):
        return pltpu.make_async_remote_copy(
            src_ref=right_at(col, seat), dst_ref=right_at(col, seat),
            send_sem=send_pair.at[col, other], recv_sem=recv_pair.at[col, seat],
            device_id=(owner * group + other, c, f), device_id_type=MESH,
        )

    def came_pair(col, other):
        return pltpu.make_async_remote_copy(
            src_ref=right_at(col, other), dst_ref=right_at(col, other),
            send_sem=send_pair.at[col, other], recv_sem=recv_pair.at[col, other],
            device_id=(r, c, f), device_id_type=MESH,
        )

    def to_col(col, i):
        part = pl.ds(pl.multiple_of(i * step, step), step)
        return pltpu.make_async_remote_copy(
            src_ref=part_out.at[col, part], dst_ref=part_in.at[c, part],
            send_sem=send_part.at[col, i], recv_sem=recv_part.at[c, i],
            device_id=(r, col, f), device_id_type=MESH,
        )

    def came_col(col, i):
        part = pl.ds(pl.multiple_of(i * step, step), step)
        return pltpu.make_async_remote_copy(
            src_ref=part_out.at[col, part], dst_ref=part_in.at[col, part],
            send_sem=send_part.at[col, i], recv_sem=recv_part.at[col, i],
            device_id=(r, col, f), device_id_type=MESH,
        )

    @pl.loop(0, CHUNKS)
    def _(i):
        @pl.when(has_down)
        def _():
            along(f, i, False).start()

        @pl.when(has_up)
        def _():
            along(f, i, True).start()

    mine = owner == c
    for t in range(n_row // group):
        @pl.when(jnp.logical_not(mine & (owner == t)))
        def _():
            to_right(t).start()

    @pl.when(mine)
    def _():
        spot = right_at(c, seat)
        spot[...] = left[f]

    def relay(d, i):
        @pl.when(f - d >= 0)
        def _():
            along(f - d, i, True).wait_recv()

            @pl.when(has_up)
            def _():
                along(f - d, i, True).start()

        @pl.when(f + d < n_fib)
        def _():
            along(f + d, i, False).wait_recv()

            @pl.when(has_down)
            def _():
                along(f + d, i, False).start()

    def gather_right():
        for col in range(n_col):
            @pl.when(jnp.logical_not(mine & (c == col)))
            def _():
                came_right(col).wait_recv()

            for other in range(group):
                @pl.when(seat != other)
                def _():
                    to_pair(col, other).start()

    for d in range(1, n_fib - 1):
        @pl.loop(0, CHUNKS)
        def _(i):
            relay(d, i)

        if d == 1:
            gather_right()
    if n_fib < 3:
        gather_right()

    for col in range(n_col):
        for other in range(group):
            @pl.when(seat != other)
            def _():
                came_pair(col, other).wait_recv()

    @pl.loop(0, CHUNKS)
    def _(i):
        if n_fib > 1:
            relay(n_fib - 1, i)
        part = pl.ds(pl.multiple_of(i * step, step), step)
        for col in range(n_col):
            product = jnp.zeros((step, unit), jnp.float32)
            for k in range(n_fib):
                product += jnp.dot(
                    left[k, part, :],
                    right[k * unit:(k + 1) * unit, col * unit:(col + 1) * unit],
                    preferred_element_type=jnp.float32,
                )

            @pl.when(c == col)
            def _():
                own[part, :] = product

            @pl.when(c != col)
            def _():
                part_out[col, part, :] = product.astype(jnp.bfloat16)
                to_col(col, i).start()

    column = jnp.zeros((8, unit), jnp.float32)
    for i in range(CHUNKS):
        at = slice(i * step, (i + 1) * step)
        for shift in range(1, n_col):
            col = lax.rem(c + shift, n_col)
            came_col(col, i).wait_recv()
            own[at, :] += part_in[col, at, :].astype(jnp.float32)
        squared = own[at, :] * own[at, :]
        own[at, :] = squared
        column += jnp.sum(squared.reshape(step // 8, 8, unit), axis=0)
    sums[r] = column

    def to_row(shift):
        return pltpu.make_async_remote_copy(
            src_ref=sums.at[r], dst_ref=sums.at[r],
            send_sem=send_sum.at[shift], recv_sem=recv_sum.at[r],
            device_id=(lax.rem(r + shift, n_row), c, f), device_id_type=MESH,
        )

    def came_row(other):
        return pltpu.make_async_remote_copy(
            src_ref=sums.at[r], dst_ref=sums.at[other],
            send_sem=send_sum.at[0], recv_sem=recv_sum.at[other],
            device_id=(other, c, f), device_id_type=MESH,
        )

    for shift in range(1, n_row):
        to_row(shift).start()
    for shift in range(1, n_row):
        came_row(lax.rem(r + shift, n_row)).wait_recv()
    total = sums[0]
    for other in range(1, n_row):
        total += sums[other]
    scale = jnp.sum(total, axis=0, keepdims=True) / (rows * n_row) + 1e-6
    inverse = 1.0 / scale
    for i in range(rows // tile):
        for j in range(unit // tile):
            at = (slice(i * tile, (i + 1) * tile), slice(j * tile, (j + 1) * tile))
            out_ref[at] = own[at] * (inverse[:, at[1]] * keep_ref[i, j].astype(jnp.float32))

    @pl.loop(0, CHUNKS)
    def _(i):
        for source in range(n_fib):
            @pl.when(has_up & (source <= f))
            def _():
                along(source, i, True).wait_send()

            @pl.when(has_down & (source >= f))
            def _():
                along(source, i, False).wait_send()

        for shift in range(1, n_col):
            to_col(lax.rem(c + shift, n_col), i).wait_send()

    for t in range(n_row // group):
        @pl.when(jnp.logical_not(mine & (owner == t)))
        def _():
            to_right(t).wait_send()

    for col in range(n_col):
        for other in range(group):
            @pl.when(seat != other)
            def _():
                to_pair(col, other).wait_send()

    for shift in range(1, n_row):
        to_row(shift).wait_send()


def solution(mesh):
    n_row, n_col, n_fib = (mesh.shape[name] for name in ("row", "col", "fiber"))
    group = n_row // n_col

    def local(values, tile_mask, keep_mask):
        rows, unit = values.shape
        dma = pltpu.SemaphoreType.DMA
        return pl.pallas_call(
            functools.partial(kernel, n_row, n_col, n_fib),
            out_shape=jax.ShapeDtypeStruct((rows, unit), jnp.float32),
            in_specs=[
                pl.BlockSpec(memory_space=pltpu.SMEM),
                pl.BlockSpec(memory_space=pltpu.SMEM),
                pl.BlockSpec(memory_space=pltpu.VMEM),
            ],
            out_specs=pl.BlockSpec(memory_space=pltpu.VMEM),
            scratch_shapes=[
                pltpu.VMEM((n_fib, rows, unit), jnp.bfloat16),
                pltpu.VMEM((group * rows, n_col * unit), jnp.bfloat16),
                pltpu.VMEM((rows, unit), jnp.float32),
                pltpu.VMEM((n_col, rows, unit), jnp.bfloat16),
                pltpu.VMEM((n_col, rows, unit), jnp.bfloat16),
                pltpu.VMEM((n_row, 8, unit), jnp.float32),
                dma((n_fib, CHUNKS)),
                dma((n_fib, CHUNKS)),
                dma((n_fib, CHUNKS)),
                dma((n_row // group,)),
                dma((n_col,)),
                dma((n_col, group)),
                dma((n_col, group)),
                dma((n_col, CHUNKS)),
                dma((n_col, CHUNKS)),
                dma((n_row,)),
                dma((n_row,)),
            ],
            compiler_params=pltpu.CompilerParams(collective_id=0, has_side_effects=True),
        )(tile_mask, keep_mask, values)

    spec = P("row", ("col", "fiber"))
    return jax.shard_map(
        local, mesh=mesh, in_specs=(spec, spec, spec), out_specs=spec, check_vma=False
    )
```

time: 150 us -> 61.1 us (0.41)
  waiting for transfers between devices: 75.3 us -> 0 us
  Pallas kernels: 0 us -> 55.8 us
  blocking collectives: 46.1 us -> 0 us
  between operations: 13.2 us -> 0.01 us
  matrix products: 4.05 us -> 0 us
  local copies, waits for them, and re-layouts: 8.19 us -> 5.06 us
  other arithmetic: 2.63 us -> 0 us
    pallas_call x0 -> x1, Pallas kernels: none -> 55.8 us  [local(): pl.pallas_call(functools.partial(kernel, n_row, n_col, n_fib), out_shape=...]
    unnamed x4 -> x0, waiting for transfers between devices: 47.2 us -> none
    all_to_all x2 -> x0, blocking collectives: 39.9 us -> none  [the longest x1 22.1 us: local(): lax.all_to_all(left_stack, 'fiber', split_axis=1, concat_axis=1, tiled=True)]
    all_gather x2 -> x0, waiting for transfers between devices: 28 us -> none  [the longest x1 25.6 us: local(): lax.all_gather(right_local, 'row', axis=0, tiled=True)]
    psum x1 -> x0, blocking collectives: 6.17 us -> none  [local(): col_total = lax.psum(jnp.sum(squared, axis=0), 'row')]
    dot_general x1 -> x0, matrix products: 4.05 us -> none  [local(): jnp.dot(left_all, lax.all_gather(right_local, 'row', axis=0, tiled=True),...]
    unnamed x7 -> x3, local copies, waits for them, and re-layouts: 5.65 us -> 5.06 us
  transfers between devices with their start and end apart: 3 -> 0, of which waited for: 3 -> 0; matrix products, arithmetic and copies ran while one was open for 1% -> 0% of each run, Pallas kernels for 0% -> 0%
where the time goes in v1:
time: 61.1 us; the launch traced here: 60.9 us
  Pallas kernels  55.8 us (91%)
  local copies, waits for them, and re-layouts  5.06 us (8%)
    pallas_call x1, Pallas kernels, local(): pl.pallas_call(functools.partial(kernel, n_row, n_col, n_fib), out_shape=...  55.8 us
    unnamed x3, local copies, waits for them, and re-layouts  5.06 us

profile of v1, /device:TPU:0, one launch (start us, length us, event | category | flops | bytes accessed | tf_op | source)
XLA Modules:
  0.0 60.9 jit_solution(18170770699954623221)
XLA Ops:
  0.0 1.4 %copy.4.tile_ref = s32[6,3]{1,0:T(8,128)} copy(s32[6,3]{0,1:T(4,128)} %param.4) | data formatting | bytes 144 | tf_op args[1]
  1.4 1.4 %copy.5.keep_ref = s32[6,3]{1,0:T(8,128)} copy(s32[6,3]{0,1:T(4,128)} %param.5) | data formatting | bytes 144 | tf_op args[2]
  2.7 55.8 %shard_map.37 = f32[768,384]{1,0:T(8,128)} custom-call(s32[6,3]{1,0:T(8,128)} %copy.4.tile_ref, s32[6,3]{1,0:T(8,128)} %copy.5.keep_ref, f32[768,384]{1,0:T(8,128)} %values_ref.1), custom_call_target="tpu_custom_call" | custom-call | tf_op jit(solution)/shard_map/pallas_call | solution.py:278
  58.6 2.4 %copy.7 = f32[768,384]{1,0:T(8,128)} copy(f32[768,384]{1,0:T(8,128)} %shard_map.37) | data formatting | bytes 2359296

commit v2 on v1

--- a/solution.py
+++ b/solution.py
@@ -8,21 +8,27 @@
 from jax.sharding import PartitionSpec as P
 
 MESH = pl.DeviceIdType.MESH
-CHUNKS = 4
+CHUNKS = 6
+VMEM_LIMIT = 62 * 1024 * 1024
 
 
 def kernel(
-    n_row, n_col, n_fib, tile_ref, keep_ref, values_ref, out_ref,
-    left, right, own, part_out, part_in, sums,
+    n_row, n_col, n_fib, tile_hbm, values_hbm, own, inverse_ref,
+    tile_ref, values_ref, left, right, part_out, part_in, sums, load_sem,
     send_up, send_down, recv_left, send_right, recv_right, send_pair, recv_pair,
     send_part, recv_part, send_sum, recv_sum,
 ):
     r, c, f = lax.axis_index("row"), lax.axis_index("col"), lax.axis_index("fiber")
     rows, unit = values_ref.shape
-    tile = unit // tile_ref.shape[1]
+    tile = unit // tile_ref.shape[0]
     step = rows // CHUNKS
     group = n_row // n_col
     owner, seat = r // group, lax.rem(r, group)
+
+    load = pltpu.make_async_copy(values_hbm, values_ref, load_sem.at[0])
+    load.start()
+    load_tile = pltpu.make_async_copy(tile_hbm, tile_ref, load_sem.at[1])
+    load_tile.start()
 
     barrier = pltpu.get_barrier_semaphore()
     for dr in range(n_row):
@@ -43,10 +49,13 @@
     def _():
         pl.semaphore_signal(barrier, inc=1, device_id=(r, c, f + 1), device_id_type=MESH)
 
+    load_tile.wait()
+    load.wait()
+
     for i in range(rows // tile):
         for j in range(unit // tile):
             at = (pl.ds(i * tile, tile), pl.ds(j * tile, tile))
-            masked = values_ref[at] * tile_ref[i, j].astype(jnp.float32)
+            masked = values_ref[at] * tile_ref[j, i].astype(jnp.float32)
             left[f, i * tile:(i + 1) * tile, j * tile:(j + 1) * tile] = masked.astype(jnp.bfloat16)
 
     neighbours = has_down.astype(jnp.int32) + has_up.astype(jnp.int32)
@@ -233,11 +242,7 @@
     for other in range(1, n_row):
         total += sums[other]
     scale = jnp.sum(total, axis=0, keepdims=True) / (rows * n_row) + 1e-6
-    inverse = 1.0 / scale
-    for i in range(rows // tile):
-        for j in range(unit // tile):
-            at = (slice(i * tile, (i + 1) * tile), slice(j * tile, (j + 1) * tile))
-            out_ref[at] = own[at] * (inverse[:, at[1]] * keep_ref[i, j].astype(jnp.float32))
+    inverse_ref[...] = jnp.broadcast_to(1.0 / scale, inverse_ref.shape)
 
     @pl.loop(0, CHUNKS)
     def _(i):
@@ -268,6 +273,22 @@
         to_row(shift).wait_send()
 
 
+def prune(keep_ref, squared_ref, inverse_ref, out_hbm, out_vmem, sem):
+    tile = out_vmem.shape[1] // keep_ref.shape[0]
+    copies = []
+    for i in range(keep_ref.shape[1]):
+        down = slice(i * tile, (i + 1) * tile)
+        for j in range(keep_ref.shape[0]):
+            across = slice(j * tile, (j + 1) * tile)
+            factor = inverse_ref[0:1, across] * keep_ref[j, i].astype(jnp.float32)
+            out_vmem[down, across] = squared_ref[down, across] * factor
+        copy = pltpu.make_async_copy(out_vmem.at[down], out_hbm.at[down], sem.at[i])
+        copy.start()
+        copies.append(copy)
+    for copy in copies:
+        copy.wait()
+
+
 def solution(mesh):
     n_row, n_col, n_fib = (mesh.shape[name] for name in ("row", "col", "fiber"))
     group = n_row // n_col
@@ -275,22 +296,29 @@
     def local(values, tile_mask, keep_mask):
         rows, unit = values.shape
         dma = pltpu.SemaphoreType.DMA
-        return pl.pallas_call(
+        squared, inverse = pl.pallas_call(
             functools.partial(kernel, n_row, n_col, n_fib),
-            out_shape=jax.ShapeDtypeStruct((rows, unit), jnp.float32),
+            out_shape=(
+                pltpu.VMEM((rows, unit), jnp.float32),
+                pltpu.VMEM((8, unit), jnp.float32),
+            ),
             in_specs=[
-                pl.BlockSpec(memory_space=pltpu.SMEM),
-                pl.BlockSpec(memory_space=pltpu.SMEM),
+                pl.BlockSpec(memory_space=pltpu.HBM),
+                pl.BlockSpec(memory_space=pltpu.HBM),
+            ],
+            out_specs=(
                 pl.BlockSpec(memory_space=pltpu.VMEM),
-            ],
-            out_specs=pl.BlockSpec(memory_space=pltpu.VMEM),
+                pl.BlockSpec(memory_space=pltpu.VMEM),
+            ),
             scratch_shapes=[
+                pltpu.SMEM(tile_mask.shape[::-1], jnp.int32),
+                pltpu.VMEM((rows, unit), jnp.float32),
                 pltpu.VMEM((n_fib, rows, unit), jnp.bfloat16),
                 pltpu.VMEM((group * rows, n_col * unit), jnp.bfloat16),
-                pltpu.VMEM((rows, unit), jnp.float32),
                 pltpu.VMEM((n_col, rows, unit), jnp.bfloat16),
                 pltpu.VMEM((n_col, rows, unit), jnp.bfloat16),
                 pltpu.VMEM((n_row, 8, unit), jnp.float32),
+                dma((2,)),
                 dma((n_fib, CHUNKS)),
                 dma((n_fib, CHUNKS)),
                 dma((n_fib, CHUNKS)),
@@ -303,8 +331,27 @@
                 dma((n_row,)),
                 dma((n_row,)),
             ],
-            compiler_params=pltpu.CompilerParams(collective_id=0, has_side_effects=True),
-        )(tile_mask, keep_mask, values)
+            compiler_params=pltpu.CompilerParams(
+                collective_id=0, has_side_effects=True, vmem_limit_bytes=VMEM_LIMIT
+            ),
+            name="expand",
+        )(tile_mask.T, values)
+        return pl.pallas_call(
+            prune,
+            out_shape=jax.ShapeDtypeStruct((rows, unit), jnp.float32),
+            in_specs=[
+                pl.BlockSpec(memory_space=pltpu.SMEM),
+                pl.BlockSpec(memory_space=pltpu.VMEM),
+                pl.BlockSpec(memory_space=pltpu.VMEM),
+            ],
+            out_specs=pl.BlockSpec(memory_space=pl.ANY),
+            scratch_shapes=[
+                pltpu.VMEM((rows, unit), jnp.float32),
+                dma((keep_mask.shape[0],)),
+            ],
+            compiler_params=pltpu.CompilerParams(vmem_limit_bytes=8 * 1024 * 1024),
+            name="prune",
+        )(keep_mask.T, squared, inverse)
 
     spec = P("row", ("col", "fiber"))
     return jax.shard_map(

time: 61.1 us -> 54.2 us (0.89)
  local copies, waits for them, and re-layouts: 5.06 us -> 0.01 us
  Pallas kernels: 55.8 us -> 54.1 us
    unnamed x3 -> x2, local copies, waits for them, and re-layouts: 5.06 us -> 0.01 us
    pallas_call x1, Pallas kernels: 55.8 us -> 52.4 us  [local(): pl.pallas_call(functools.partial(kernel, n_row, n_col, n_fib), out_shape=...]
    pallas_call x0 -> x1, Pallas kernels: none -> 1.64 us  [local(): pl.pallas_call(prune, out_shape=jax.ShapeDtypeStruct((rows, unit), jnp.fl...]
where the time goes in v2:
time: 54.2 us; the launch traced here: 54.1 us
  Pallas kernels  54.1 us (100%)
    pallas_call x1, Pallas kernels, local(): pl.pallas_call(functools.partial(kernel, n_row, n_col, n_fib), out_shape=...  52.4 us
    pallas_call x1, Pallas kernels, local(): pl.pallas_call(prune, out_shape=jax.ShapeDtypeStruct((rows, unit), jnp.fl...  1.64 us

profile of v2, /device:TPU:0, one launch (start us, length us, event | category | flops | bytes accessed | tf_op | source)
XLA Modules:
  0.0 54.1 jit_solution(10720935636312854162)
XLA Ops:
  0.0 0.0 copy-start
  0.0 52.4 %expand.1 = (f32[768,384]{1,0:T(8,128)S(1)}, f32[8,384]{1,0:T(8,128)S(1)}) custom-call(s32[3,6]{1,0:T(4,128)} %bitcast.3, f32[768,384]{1,0:T(8,128)} %values_hbm.1), custom_call_target="tpu_custom_call" | custom-call | tf_op jit(solution)/shard_map/expand/pallas_call | solution.py:299
  52.5 0.0 copy-done
  52.5 1.6 %prune.1 = f32[768,384]{1,0:T(8,128)} custom-call(s32[3,6]{1,0:T(4,128)S(1)} %bitcast.2, f32[768,384]{1,0:T(8,128)S(1)} %get-tuple-element.7.squared_ref, f32[8,384]{1,0:T(8,128)S(1)} %get-tuple-element.8.inverse_ref), custom_call_target="tpu_custom_call" | custom-call | tf_op jit(solution)/shard_map/prune/pallas_call | solution.py:339
Async XLA Ops:
  0.0 52.5 %copy-start = (s32[6,3]{0,1:T(4,128)S(1)}, s32[6,3]{0,1:T(4,128)}, u32[]{:S(2)}) copy-start(s32[6,3]{0,1:T(4,128)} %param.5) | copy-start | bytes 220

commit v3 on v2

--- a/solution.py
+++ b/solution.py
@@ -9,12 +9,15 @@
 
 MESH = pl.DeviceIdType.MESH
 CHUNKS = 6
+EARLY = 3
+BLOCKS = 3
+LAG = 2
 VMEM_LIMIT = 62 * 1024 * 1024
 
 
 def kernel(
     n_row, n_col, n_fib, tile_hbm, values_hbm, own, inverse_ref,
-    tile_ref, values_ref, left, right, part_out, part_in, sums, load_sem,
+    tile_ref, values_ref, left, right, ahead, part_out, part_in, sums, load_sem,
     send_up, send_down, recv_left, send_right, recv_right, send_pair, recv_pair,
     send_part, recv_part, send_sum, recv_sum,
 ):
@@ -169,15 +172,27 @@
                 def _():
                     to_pair(col, other).start()
 
-    for d in range(1, n_fib - 1):
-        @pl.loop(0, CHUNKS)
-        def _(i):
-            relay(d, i)
-
-        if d == 1:
-            gather_right()
-    if n_fib < 3:
-        gather_right()
+    up_late, down_late = f + 1 == n_fib - 1, f - 1 == 0
+
+    @pl.loop(0, CHUNKS)
+    def _(i):
+        @pl.when(has_down)
+        def _():
+            along(f - 1, i, True).wait_recv()
+
+            @pl.when(has_up & (jnp.logical_not(up_late) | (i < EARLY)))
+            def _():
+                along(f - 1, i, True).start()
+
+        @pl.when(has_up)
+        def _():
+            along(f + 1, i, False).wait_recv()
+
+            @pl.when(has_down & (jnp.logical_not(down_late) | (i < EARLY)))
+            def _():
+                along(f + 1, i, False).start()
+
+    gather_right()
 
     for col in range(n_col):
         for other in range(group):
@@ -185,40 +200,79 @@
             def _():
                 came_pair(col, other).wait_recv()
 
-    @pl.loop(0, CHUNKS)
-    def _(i):
-        if n_fib > 1:
-            relay(n_fib - 1, i)
+    first = jnp.where(has_down, f - 1, 0)
+    ready = min(n_fib, 2)
+
+    def product(part, shift, k):
+        col = lax.rem(c + shift, n_col)
+        return jnp.dot(
+            left[k, part, :],
+            right[
+                pl.ds(pl.multiple_of(k * unit, unit), unit),
+                pl.ds(pl.multiple_of(col * unit, unit), unit),
+            ],
+            preferred_element_type=jnp.float32,
+        )
+
+    def total_at(shift):
+        return own if shift == 0 else ahead.at[shift - 1]
+
+    @pl.loop(0, BLOCKS)
+    def _(i):
+        part = pl.ds(pl.multiple_of(i * (rows // BLOCKS), rows // BLOCKS), rows // BLOCKS)
+        for shift in range(n_col):
+            total = jnp.zeros((rows // BLOCKS, unit), jnp.float32)
+            for k in range(ready):
+                total += product(part, shift, lax.rem(first + k, n_fib))
+            total_at(shift)[part, :] = total
+
+    sums[r] = jnp.zeros((8, unit), jnp.float32)
+
+    def combine(i):
         part = pl.ds(pl.multiple_of(i * step, step), step)
-        for col in range(n_col):
-            product = jnp.zeros((step, unit), jnp.float32)
-            for k in range(n_fib):
-                product += jnp.dot(
-                    left[k, part, :],
-                    right[k * unit:(k + 1) * unit, col * unit:(col + 1) * unit],
-                    preferred_element_type=jnp.float32,
-                )
-
-            @pl.when(c == col)
-            def _():
-                own[part, :] = product
-
-            @pl.when(c != col)
-            def _():
-                part_out[col, part, :] = product.astype(jnp.bfloat16)
-                to_col(col, i).start()
-
-    column = jnp.zeros((8, unit), jnp.float32)
-    for i in range(CHUNKS):
-        at = slice(i * step, (i + 1) * step)
+        expanded = own[part, :]
         for shift in range(1, n_col):
             col = lax.rem(c + shift, n_col)
             came_col(col, i).wait_recv()
-            own[at, :] += part_in[col, at, :].astype(jnp.float32)
-        squared = own[at, :] * own[at, :]
-        own[at, :] = squared
-        column += jnp.sum(squared.reshape(step // 8, 8, unit), axis=0)
-    sums[r] = column
+            expanded += part_in[col, part, :].astype(jnp.float32)
+        squared = expanded * expanded
+        own[part, :] = squared
+        sums[r] += jnp.sum(squared.reshape(step // 8, 8, unit), axis=0)
+
+    @pl.loop(0, CHUNKS)
+    def _(i):
+        @pl.when(has_up & has_down & (i < CHUNKS - EARLY))
+        def _():
+            @pl.when(up_late)
+            def _():
+                along(f - 1, i + EARLY, True).start()
+
+            @pl.when(down_late)
+            def _():
+                along(f + 1, i + EARLY, False).start()
+
+        for d in range(2, n_fib):
+            relay(d, i)
+        part = pl.ds(pl.multiple_of(i * step, step), step)
+        for shift in range(1, n_col):
+            col = lax.rem(c + shift, n_col)
+            total = ahead[shift - 1, part, :]
+            for k in range(ready, n_fib):
+                total += product(part, shift, lax.rem(first + k, n_fib))
+            part_out[col, part, :] = total.astype(jnp.bfloat16)
+            to_col(col, i).start()
+        total = own[part, :]
+        for k in range(ready, n_fib):
+            total += product(part, 0, lax.rem(first + k, n_fib))
+        own[part, :] = total
+
+        @pl.when(i >= LAG)
+        def _():
+            combine(i - LAG)
+
+    @pl.loop(CHUNKS - LAG, CHUNKS)
+    def _(i):
+        combine(i)
 
     def to_row(shift):
         return pltpu.make_async_remote_copy(
@@ -315,6 +369,7 @@
                 pltpu.VMEM((rows, unit), jnp.float32),
                 pltpu.VMEM((n_fib, rows, unit), jnp.bfloat16),
                 pltpu.VMEM((group * rows, n_col * unit), jnp.bfloat16),
+                pltpu.VMEM((n_col - 1, rows, unit), jnp.float32),
                 pltpu.VMEM((n_col, rows, unit), jnp.bfloat16),
                 pltpu.VMEM((n_col, rows, unit), jnp.bfloat16),
                 pltpu.VMEM((n_row, 8, unit), jnp.float32),

time: 54.2 us -> 53.2 us (0.982)
  Pallas kernels: 54.1 us -> 53 us
    pallas_call x1, Pallas kernels: 52.4 us -> 51.4 us  [local(): pl.pallas_call(functools.partial(kernel, n_row, n_col, n_fib), out_shape=...]
where the time goes in v3:
time: 53.2 us; the launch traced here: 53 us
  Pallas kernels  53 us (100%)
    pallas_call x1, Pallas kernels, local(): pl.pallas_call(functools.partial(kernel, n_row, n_col, n_fib), out_shape=...  51.4 us
    pallas_call x1, Pallas kernels, local(): pl.pallas_call(prune, out_shape=jax.ShapeDtypeStruct((rows, unit), jnp.fl...  1.64 us

profile of v3, /device:TPU:0, one launch (start us, length us, event | category | flops | bytes accessed | tf_op | source)
XLA Modules:
  0.0 53.0 jit_solution(5466376979949230586)
XLA Ops:
  0.0 0.0 copy-start
  0.0 51.4 %expand.1 = (f32[768,384]{1,0:T(8,128)S(1)}, f32[8,384]{1,0:T(8,128)S(1)}) custom-call(s32[3,6]{1,0:T(4,128)} %bitcast.3, f32[768,384]{1,0:T(8,128)} %values_hbm.1), custom_call_target="tpu_custom_call" | custom-call | tf_op jit(solution)/shard_map/expand/pallas_call | solution.py:353
  51.4 0.0 copy-done
  51.4 1.6 %prune.1 = f32[768,384]{1,0:T(8,128)} custom-call(s32[3,6]{1,0:T(4,128)S(1)} %bitcast.2, f32[768,384]{1,0:T(8,128)S(1)} %get-tuple-element.7.squared_ref, f32[8,384]{1,0:T(8,128)S(1)} %get-tuple-element.8.inverse_ref), custom_call_target="tpu_custom_call" | custom-call | tf_op jit(solution)/shard_map/prune/pallas_call | solution.py:394
Async XLA Ops:
  0.0 51.4 %copy-start = (s32[6,3]{0,1:T(4,128)S(1)}, s32[6,3]{0,1:T(4,128)}, u32[]{:S(2)}) copy-start(s32[6,3]{0,1:T(4,128)} %param.5) | copy-start | bytes 220

commit v4 on v3

--- a/solution.py
+++ b/solution.py
@@ -241,18 +241,19 @@
 
     @pl.loop(0, CHUNKS)
     def _(i):
-        @pl.when(has_up & has_down & (i < CHUNKS - EARLY))
-        def _():
-            @pl.when(up_late)
-            def _():
-                along(f - 1, i + EARLY, True).start()
-
-            @pl.when(down_late)
-            def _():
-                along(f + 1, i + EARLY, False).start()
-
         for d in range(2, n_fib):
             relay(d, i)
+
+        @pl.when(has_up & has_down & (i < CHUNKS - EARLY))
+        def _():
+            @pl.when(up_late)
+            def _():
+                along(f - 1, i + EARLY, True).start()
+
+            @pl.when(down_late)
+            def _():
+                along(f + 1, i + EARLY, False).start()
+
         part = pl.ds(pl.multiple_of(i * step, step), step)
         for shift in range(1, n_col):
             col = lax.rem(c + shift, n_col)

time: 53.2 us -> 53.2 us (level)
  no operation moved by 1% of the time
where the time goes in v4:
time: 53.2 us; the launch traced here: 53 us
  Pallas kernels  53 us (100%)
    pallas_call x1, Pallas kernels, local(): pl.pallas_call(functools.partial(kernel, n_row, n_col, n_fib), out_shape=...  51.4 us
    pallas_call x1, Pallas kernels, local(): pl.pallas_call(prune, out_shape=jax.ShapeDtypeStruct((rows, unit), jnp.fl...  1.64 us

profile of v4, /device:TPU:0, one launch (start us, length us, event | category | flops | bytes accessed | tf_op | source)
XLA Modules:
  0.0 53.0 jit_solution(6889683736838353108)
XLA Ops:
  0.0 0.0 copy-start
  0.0 51.4 %expand.1 = (f32[768,384]{1,0:T(8,128)S(1)}, f32[8,384]{1,0:T(8,128)S(1)}) custom-call(s32[3,6]{1,0:T(4,128)} %bitcast.3, f32[768,384]{1,0:T(8,128)} %values_hbm.1), custom_call_target="tpu_custom_call" | custom-call | tf_op jit(solution)/shard_map/expand/pallas_call | solution.py:354
  51.4 0.0 copy-done
  51.4 1.6 %prune.1 = f32[768,384]{1,0:T(8,128)} custom-call(s32[3,6]{1,0:T(4,128)S(1)} %bitcast.2, f32[768,384]{1,0:T(8,128)S(1)} %get-tuple-element.7.squared_ref, f32[8,384]{1,0:T(8,128)S(1)} %get-tuple-element.8.inverse_ref), custom_call_target="tpu_custom_call" | custom-call | tf_op jit(solution)/shard_map/prune/pallas_call | solution.py:395
Async XLA Ops:
  0.0 51.4 %copy-start = (s32[6,3]{0,1:T(4,128)S(1)}, s32[6,3]{0,1:T(4,128)}, u32[]{:S(2)}) copy-start(s32[6,3]{0,1:T(4,128)} %param.5) | copy-start | bytes 220
